TPU v7x, 32 devices: a whole 2x2x4 slice. The times are simulated.
32 devices in a mesh: sector: 8 (over z, x), mpo: 4 (over y, core).
Axes of the slice: x: 2, y: 2, z: 4, core: 2. Of those that a mesh axis runs over, the one named last changes fastest.
Arguments:
- psi: float32 [8, 768, 768], P('sector'), may hold values from -24 to 24, as said below
- left_env: float32 [4, 8, 768, 768], P('mpo', 'sector'), may hold values from -0.21875 to 0.21875
- right_env: float32 [4, 8, 768, 768], P('mpo', 'sector'), may hold values from -0.21875 to 0.21875
- sector_label: int32 [8], replicated, may hold values from 0 to 7, as said below
- charge_step: int32 [4, 8, 3], replicated, may hold values from -1 to 1
- coef_index: int32 [4, 8, 3], replicated, may hold values from 0 to 7
- entry_values: float32 [8], replicated, may hold values from -1.5 to 1.5
- recurrence: float32 [3], replicated, may hold values from -2 to 2
Outputs:
- vec_one: float32 [8, 768, 768], P('sector')
- vec_two: float32 [8, 768, 768], P('sector')
Inputs may be any that keep to these rules, and one draw needn't show every extreme that they name: `psi`: each sector block's entries lie in this range. `sector_label`: A permutation of the labels over the slots; two sectors whose labels differ by one lie at most 3 slots apart.
All inputs are finite; a program needn't handle non-finite values.
Results may differ from a plain program's by a relative error of at most 0.0029.
Values may be sent and summed in bfloat16 or wider, within the bound.
A program may use at most 64 MiB of HBM per device.

v0:
```python
import functools

import jax
import jax.numpy as jnp
from jax import lax
from jax.experimental import pallas as pl
from jax.experimental.pallas import tpu as pltpu
from jax.sharding import PartitionSpec as P

EPS = 1e-06
LEAN_CHUNKS, FULL_CHUNKS = 6, 3
FROM_PARTNER, FROM_BELOW, FROM_ABOVE, PARTNER_RELAY, ABOVE_RELAY, BELOW_RELAY = range(6)
MESH = pl.DeviceIdType.MESH
f32, bf16 = jnp.float32, jnp.bfloat16


def split(value):
    high = value.astype(bf16)
    return high, (value - high.astype(f32)).astype(bf16)


def dot_split(left, right_high, right_low):
    high, low = split(left)
    dot = functools.partial(jnp.dot, preferred_element_type=f32)
    return dot(high, right_high) + (dot(low, right_high) + dot(high, right_low))


def kernel(
    lean, chunks, sectors, bonds, cells,
    label_ref, step_ref, index_ref, entry_ref, coef_ref, left_ref, right_ref, psi_ref,
    one_ref, two_ref,
    hi, lo, right_hi, right_lo, own, pick, slots, term, half_in, half, part_in, resid, squares, parts, sums,
    x_send, x_recv, p_send, p_recv, y_send, y_recv, g_send, g_recv, h_send, h_recv, q_send, q_recv, s_send, s_recv,
):
    sector, bond = lax.axis_index("sector"), lax.axis_index("mpo")
    width = left_ref.shape[0]
    rows = width // chunks
    pair_rows = rows // 2
    stacks = bonds // 2
    part_rows = pair_rows // stacks
    core, stack = lax.rem(bond, 2), bond // 2
    sign = 1 - 2 * lax.rem(sector, 2)
    partner, ahead, behind = sector + sign, sector + 2 * sign, sector - 2 * sign
    has_ahead = (ahead >= 0) & (ahead < sectors)
    has_behind = (behind >= 0) & (behind < sectors)
    has_far = (sector - 4 * sign >= 0) & (sector - 4 * sign < sectors)
    other_core = stack * 2 + 1 - core
    entries = step_ref.shape[0]

    def stack_at(step):
        return lax.rem(stack + step, stacks) * 2 + core

    barrier = pltpu.get_barrier_semaphore()
    for step in range(1, sectors):
        pl.semaphore_signal(
            barrier, inc=1, device_id=(lax.rem(sector + step, sectors), bond), device_id_type=MESH
        )
    for step in range(1, bonds):
        pl.semaphore_signal(
            barrier, inc=1, device_id=(sector, lax.rem(bond + step, bonds)), device_id_type=MESH
        )

    def inside(slot):
        return jnp.minimum(jnp.maximum(slot, 0), sectors - 1)

    own_label = label_ref[sector]

    def couple(source):
        slot = inside(source)
        label = label_ref[slot]
        total = f32(0.0)
        for entry in range(entries):
            match = label + step_ref[entry, bond, slot] == own_label
            value = entry_ref[index_ref[entry, bond, slot]]
            total = total + jnp.where(match, value, f32(0.0))
        return jnp.where(source == slot, total, f32(0.0))

    def adjacent(slot):
        gap = label_ref[inside(slot)] - own_label
        return (gap == 1) | (gap == -1)

    own_weight = couple(sector)
    if lean:
        takes = (jnp.where(adjacent(ahead), f32(1.0), f32(0.0)),
                 jnp.where(adjacent(behind), f32(1.0), f32(0.0)))
        weights = (
            couple(partner),
            jnp.where(adjacent(behind), couple(behind), couple(behind + sign)),
            jnp.where(adjacent(ahead), couple(ahead), couple(ahead + sign)),
        )
    else:
        weights = tuple(couple(sector + sign * place) for place in (1, -2, 2, -1, 3, -3))

    def send(source, target, send_sem, recv_sem, device):
        return pltpu.make_async_remote_copy(
            src_ref=source, dst_ref=target, send_sem=send_sem, recv_sem=recv_sem,
            device_id=device, device_id_type=MESH,
        )

    def block_copy(kind, c):
        here = pl.ds(pl.multiple_of(c * rows, rows), rows)
        source, device = {
            FROM_PARTNER: (own, partner),
            FROM_BELOW: (pick.at[0] if lean else own, ahead),
            FROM_ABOVE: (pick.at[1] if lean else own, behind),
            PARTNER_RELAY: (slots.at[FROM_ABOVE], partner),
            ABOVE_RELAY: (slots.at[FROM_PARTNER], behind),
            BELOW_RELAY: (slots.at[min(PARTNER_RELAY, len(weights) - 1)], ahead),
        }[kind]
        return send(
            source.at[here], slots.at[kind, here], x_send.at[kind, c], x_recv.at[kind, c],
            (device, bond),
        )

    sends_if = {
        FROM_PARTNER: None, FROM_BELOW: has_ahead, FROM_ABOVE: has_behind,
        PARTNER_RELAY: has_ahead, ABOVE_RELAY: has_behind, BELOW_RELAY: has_ahead & has_behind,
    }
    gets_if = {
        FROM_PARTNER: None, FROM_BELOW: has_behind, FROM_ABOVE: has_ahead,
        PARTNER_RELAY: has_behind, ABOVE_RELAY: has_ahead, BELOW_RELAY: has_far,
    }

    def when(condition, action):
        if condition is None:
            action()
        else:
            pl.when(condition)(action)

    def start(kind, c):
        when(sends_if[kind], lambda: block_copy(kind, c).start())

    def arrive(kind, c):
        when(gets_if[kind], lambda: block_copy(kind, c).wait_recv())

    def pair_copy(c):
        there = c * rows + (1 - core) * pair_rows
        there = pl.ds(pl.multiple_of(there, 8), pair_rows)
        return send(
            term.at[there], half_in.at[c], p_send.at[c], p_recv.at[c], (sector, other_core)
        )

    def stack_copy(c, step):
        there = pl.ds(pl.multiple_of(lax.rem(stack + step, stacks) * part_rows, 8), part_rows)
        return send(
            half.at[c, there], part_in.at[c, step - 1], y_send.at[c, step - 1],
            y_recv.at[c, step - 1], (sector, stack_at(step)),
        )

    def part_at(c):
        first = c * rows + core * pair_rows + stack * part_rows
        return pl.ds(pl.multiple_of(first, 8), part_rows)

    def give_stack(c, step):
        here = part_at(c)
        return send(
            resid.at[here], resid.at[here], g_send.at[c, step - 1], g_recv.at[c, step - 1],
            (sector, stack_at(step)),
        )

    def give_pair(c):
        here = pl.ds(pl.multiple_of(c * rows + core * pair_rows, 8), pair_rows)
        return send(
            resid.at[here], resid.at[here], h_send.at[c], h_recv.at[c], (sector, other_core)
        )

    def apply(turn, vec_ref, out_ref):
        hi[...], lo[...] = split(vec_ref[...])
        if turn == 0:
            pl.semaphore_wait(barrier, sectors + bonds - 2)

        def make(c, carry):
            here = pl.ds(pl.multiple_of(c * rows, rows), rows)
            own[here, :] = dot_split(left_ref[here, :], hi[...], lo[...]).astype(bf16)
            start(FROM_PARTNER, c)
            if not lean:
                start(FROM_BELOW, c)
                start(FROM_ABOVE, c)
            return carry

        lax.fori_loop(0, chunks, make, 0)
        if turn == 0:
            right_hi[...], right_lo[...] = split(right_ref[...])

        def forward(c):
            arrive(FROM_PARTNER, c)
            if lean:
                here = pl.ds(pl.multiple_of(c * rows, rows), rows)
                mine = own[here, :].astype(f32)
                theirs = slots[FROM_PARTNER, here, :].astype(f32)
                for kind, take in zip((FROM_BELOW, FROM_ABOVE), takes):
                    value = mine * take + theirs * (1.0 - take)
                    pick[kind - FROM_BELOW, here, :] = value.astype(bf16)
                    start(kind, c)
            else:
                start(ABOVE_RELAY, c)
                arrive(FROM_ABOVE, c)
                start(PARTNER_RELAY, c)

        def forward_far(c):
            arrive(PARTNER_RELAY, c)
            start(BELOW_RELAY, c)

        def mix(c):
            here = pl.ds(pl.multiple_of(c * rows, rows), rows)
            for kind in (FROM_BELOW, FROM_ABOVE) if lean else (FROM_BELOW, ABOVE_RELAY, BELOW_RELAY):
                arrive(kind, c)
            mixed = own_weight * own[here, :].astype(f32)
            term[here, :] = mixed + weights[0] * slots[FROM_PARTNER, here, :].astype(f32)
            for kind in range(1, len(weights)):

                def add(kind=kind):
                    term[here, :] += weights[kind] * slots[kind, here, :].astype(f32)

                when(gets_if[kind], add)
            term[here, :] = dot_split(term[here, :], right_hi[...], right_lo[...])
            pair_copy(c).start()

        def reduce_pair(c):
            pair_copy(c).wait_recv()
            mine = pl.ds(pl.multiple_of(c * rows + core * pair_rows, 8), pair_rows)
            half[c] = term[mine, :] + half_in[c]
            for step in range(1, stacks):
                stack_copy(c, step).start()

        def reduce_stack(c):
            mine = pl.ds(pl.multiple_of(stack * part_rows, 8), part_rows)
            total = half[c, mine, :]
            for step in range(1, stacks):
                stack_copy(c, step).wait_recv()
                total = total + part_in[c, step - 1]
            here = part_at(c)
            total = total - coef_ref[turn] * vec_ref[here, :]
            if turn == 1:
                total = total - coef_ref[2] * psi_ref[here, :]
            resid[here, :] = total
            for step in range(1, stacks):
                give_stack(c, step).start()
            square = jnp.sum((total * total).reshape(part_rows // 8, 8, width), axis=0)
            folded = squares[...]
            for lane in range(0, width, 128):
                folded = folded + square[:, lane : lane + 128]
            squares[...] = folded

            @pl.when(c == chunks - 1)
            def _():
                parts[turn, bond] = squares[...]
                for step in range(1, bonds):
                    part_copy(step).start()

        def part_copy(step):
            return send(
                parts.at[turn, bond], parts.at[turn, bond],
                q_send.at[turn, step - 1], q_recv.at[turn, step - 1],
                (sector, lax.rem(bond + step, bonds)),
            )

        def gather_pair(c):
            for step in range(1, stacks):
                give_stack(c, step).wait_recv()
            give_pair(c).start()

        stages = [forward] + ([] if lean else [forward_far])
        stages += [mix, reduce_pair, reduce_stack, gather_pair]

        def advance(c, carry):
            for late, action in enumerate(stages):
                pl.when((c >= late) & (c < chunks + late))(
                    functools.partial(action, c - late)
                )
            return carry

        squares[...] = jnp.zeros_like(squares)
        lax.fori_loop(0, chunks + len(stages) - 1, advance, 0)

        for step in range(1, bonds):
            part_copy(step).wait_recv()
        sums[turn, sector] = jnp.sum(parts[turn], axis=0)

        def sum_copy(step):
            return send(
                sums.at[turn, sector], sums.at[turn, sector],
                s_send.at[turn, step - 1], s_recv.at[turn, step - 1],
                (lax.rem(sector + step, sectors), bond),
            )

        for c in range(chunks):
            for kind in range(len(weights)):
                when(sends_if[kind], lambda kind=kind: block_copy(kind, c).wait_send())
        for step in range(1, sectors):
            sum_copy(step).start()
        for step in range(1, bonds):
            part_copy(step).wait_send()
        for c in range(chunks):
            give_pair(c).wait_recv()
            pair_copy(c).wait_send()
            for step in range(1, stacks):
                stack_copy(c, step).wait_send()
                give_stack(c, step).wait_send()
            give_pair(c).wait_send()
        for step in range(1, sectors):
            sum_copy(step).wait_recv()
        total = jnp.sum(sums[turn], axis=0)
        total = jnp.sum(jnp.sum(total, axis=0, keepdims=True), axis=1, keepdims=True)
        scale = 1.0 / jnp.sqrt(total / cells + EPS)
        for c in range(chunks):
            here = pl.ds(c * rows, rows)
            out_ref[here, :] = resid[here, :] * scale
        for step in range(1, sectors):
            sum_copy(step).wait_send()

    apply(0, psi_ref, one_ref)
    apply(1, one_ref, two_ref)


def both(lean, sectors, bonds, operands):
    width = operands[-1].shape[0]
    chunks = LEAN_CHUNKS if lean else FULL_CHUNKS
    kinds = 3 if lean else 6
    rows = width // chunks
    far = max(bonds // 2 - 1, 1)
    dma = pltpu.SemaphoreType.DMA
    smem = pl.BlockSpec(memory_space=pltpu.SMEM)
    vmem = pl.BlockSpec(memory_space=pltpu.VMEM)
    cells = float(sectors * width * width)
    block = jax.ShapeDtypeStruct((width, width), f32)
    half_block = pltpu.VMEM((width, width), bf16)
    return pl.pallas_call(
        functools.partial(kernel, lean, chunks, sectors, bonds, cells),
        out_shape=(block, block),
        in_specs=[smem] * 5 + [vmem] * 3,
        out_specs=(vmem, vmem),
        scratch_shapes=[
            half_block, half_block, half_block, half_block, half_block,
            pltpu.VMEM((2, width, width) if lean else (1, 16, 128), bf16),
            pltpu.VMEM((kinds, width, width), bf16),
            pltpu.VMEM((width, width), f32),
            pltpu.VMEM((chunks, rows // 2, width), f32),
            pltpu.VMEM((chunks, rows // 2, width), f32),
            pltpu.VMEM((chunks, far, rows // bonds, width), f32),
            pltpu.VMEM((width, width), f32),
            pltpu.VMEM((8, 128), f32),
            pltpu.VMEM((2, bonds, 8, 128), f32),
            pltpu.VMEM((2, sectors, 8, 128), f32),
            dma((kinds, chunks)), dma((kinds, chunks)),
            dma((chunks,)), dma((chunks,)),
            dma((chunks, far)), dma((chunks, far)),
            dma((chunks, far)), dma((chunks, far)),
            dma((chunks,)), dma((chunks,)),
            dma((2, bonds - 1)), dma((2, bonds - 1)),
            dma((2, sectors - 1)), dma((2, sectors - 1)),
        ],
        compiler_params=pltpu.CompilerParams(
            collective_id=int(lean), has_side_effects=True, vmem_limit_bytes=60 * 2**20
        ),
        name="lean" if lean else "full",
    )(*operands)


def one_block_per_plane(sector_label):
    sectors = sector_label.shape[0]
    slot = jnp.arange(sectors, dtype=jnp.int32)
    twin = jnp.where(slot % 2 == 0, jnp.roll(sector_label, -1), jnp.roll(sector_label, 1))
    adjacent = jnp.abs(sector_label[:, None] - sector_label[None, :]) == 1
    other = jnp.abs(sector_label[:, None] - twin[None, :]) == 1
    gap = jnp.abs(slot[:, None] // 2 - slot[None, :] // 2)
    return ~jnp.any((adjacent & (gap > 1)) | (adjacent & other & (gap == 1)))


def local(
    sectors, bonds,
    psi, left_env, right_env, sector_label, charge_step, coef_index, entry_values, recurrence,
):
    operands = (
        sector_label, charge_step.transpose(2, 0, 1), coef_index.transpose(2, 0, 1), entry_values, recurrence,
        left_env[0, 0], right_env[0, 0], psi[0],
    )
    vec_one, vec_two = lax.cond(
        one_block_per_plane(sector_label),
        lambda: both(True, sectors, bonds, operands),
        lambda: both(False, sectors, bonds, operands),
    )
    return (vec_one[None], vec_two[None])


def solution(mesh):
    in_specs = (
        P("sector", None, None),
        P("mpo", "sector", None, None),
        P("mpo", "sector", None, None),
        P(),
        P(),
        P(),
        P(),
        P(),
    )
    out_specs = (P("sector", None, None), P("sector", None, None))
    body = functools.partial(local, mesh.shape["sector"], mesh.shape["mpo"])
    return jax.shard_map(body, mesh=mesh, in_specs=in_specs, out_specs=out_specs, check_vma=False)
```

profile of v0, /device:TPU:0, one launch (start us, length us, event | category | flops | bytes accessed | tf_op | source)
XLA Modules:
  0.0 123.8 jit_solution(1926808989297867273)
XLA Ops:
  0.6 1.3 %fusion.7 = (s32[1]{0:T(128)}, s32[1]{0:T(128)}) fusion(s32[8]{0:T(128)} %param.13), kind=kLoop, calls=%fused_computation.16 | loop fusion | bytes 16 | tf_op jit(solution)/shard_map/jit(_roll_static)/slice | solution.py:363
  1.9 0.8 fusion.8
  2.7 1.4 %compare_select_fusion = (s32[8]{0:T(128)S(1)}, s32[8]{0:T(128)S(1)}) fusion(s32[1]{0:T(128)} %get-tuple-element.64, s32[7]{0:T(128)S(1)} %get-tuple-element.66, s32[7]{0:T(128)S(1)} %get-tuple-element.65, s32[1]{0:T(128)} %get-tuple-element.63), kind=kLoop, calls=%fused_computation.10 | loop fusion | flops 128 | bytes 128 | tf_op jit(solution)/shard_map/jit(_where)/select_n | solution.py:363
  4.1 1.4 %fusion.6 = pred[]{:T(512)} fusion(s32[8]{0:T(128)S(1)} %get-tuple-element.67, s32[8]{0:T(128)S(1)} %get-tuple-element.68, s32[8]{0:T(128)} %param.13), kind=kLoop, calls=%fused_computation.9 | loop fusion | flops 959 | bytes 97 | tf_op jit(solution)/shard_map/reduce_or | solution.py:367
  6.2 113.6 %conditional.1 = ((f32[768,768]{1,0:T(8,128)S(1)}, f32[768,768]{1,0:T(8,128)})) conditional(s32[]{:T(128)} %convert_element_type.3, (s32[8]{0:T(128)}, s32[3,4,8]{2,1,0:T(4,128)}, s32[3,4,8]{2,1,0:T(4,128)}, f32[8]{0:T(128)}, f32[3]{0:T(128)}, /*index=5*/f32[768,768]{1,0:T(8,128)}, f32[768,768]{1,0:T(8,128)}, f32[768,768]{1,0:T(8,128)}) %tuple.40, ...), branch_computations={%region_1.2_spmd, %region_2.3_spmd} | conditional | bytes 8 | solution.py:378
  6.2 113.6 %lean.1 = (f32[768,768]{1,0:T(8,128)S(1)}, f32[768,768]{1,0:T(8,128)}) custom-call(s32[8]{0:T(128)} %get-tuple-element.48.label_ref, s32[3,4,8]{2,1,0:T(4,128)} %get-tuple-element.49.step_ref, s32[3,4,8]{2,1,0:T(4,128)} %get-tuple-element.50.index_ref, f32[8]{0:T(128)} %get-tuple-element.51.entry_ref, f32[3]{0:T(128)} %get-tuple-element.52.coef_ref, ...), custom_call_target="tpu_custom_call" | custom-call | tf_op jit(solution)/shard_map/cond/branch_1_fun/lean/pallas_call | solution.py:328
  119.8 0.0 copy-start
  119.9 1.4 %copy.16 = f32[1,768,768]{2,1,0:T(8,128)} copy(f32[1,768,768]{2,1,0:T(8,128)S(1)} %bitcast.13) | data formatting | bytes 4718592
  121.3 1.1 copy-done
  122.4 1.4 %copy.17 = f32[1,768,768]{2,1,0:T(8,128)} copy(f32[1,768,768]{2,1,0:T(8,128)S(1)} %bitcast.14) | data formatting | bytes 4718592
Async XLA Ops:
  119.8 2.5 %copy-start = (f32[768,768]{1,0:T(8,128)S(1)}, f32[768,768]{1,0:T(8,128)}, u32[]{:S(2)}) copy-start(f32[768,768]{1,0:T(8,128)} %get-tuple-element.61) | copy-start | bytes 7077892
where the time goes:
time: 124 us
  Pallas kernels  114 us (92%)
  local copies, waits for them, and re-layouts  6.03 us (5%)
  other arithmetic  2.81 us (2%)
  between operations  1.3 us (1%)
    pallas_call x1, Pallas kernels, both(): pl.pallas_call(functools.partial(kernel, lean, chunks, sectors, bonds, ce...  114 us
    unnamed x4, local copies, waits for them, and re-layouts  3.91 us

commit v1 on v0

--- a/solution.py
+++ b/solution.py
@@ -8,7 +8,7 @@
 from jax.sharding import PartitionSpec as P
 
 EPS = 1e-06
-LEAN_CHUNKS, FULL_CHUNKS = 6, 3
+LINK_CHUNKS, FULL_CHUNKS, LOADS = 12, 3, 6
 FROM_PARTNER, FROM_BELOW, FROM_ABOVE, PARTNER_RELAY, ABOVE_RELAY, BELOW_RELAY = range(6)
 MESH = pl.DeviceIdType.MESH
 f32, bf16 = jnp.float32, jnp.bfloat16
@@ -315,7 +315,7 @@
 
 def both(lean, sectors, bonds, operands):
     width = operands[-1].shape[0]
-    chunks = LEAN_CHUNKS if lean else FULL_CHUNKS
+    chunks = FULL_CHUNKS
     kinds = 3 if lean else 6
     rows = width // chunks
     far = max(bonds // 2 - 1, 1)
@@ -357,14 +357,330 @@
     )(*operands)
 
 
+def lean_kernel(
+    chunks, sectors, bonds, cells,
+    label_ref, step_ref, index_ref, entry_ref, coef_ref, left_hbm, right_hbm, psi_hbm,
+    one_ref, two_ref,
+    left, right, psi, hi, lo, right_hi, right_lo, own, pick, slots, term, half_in, parts, resid, squares, sums,
+    in_sem, x_send, x_recv, p_send, p_recv, y_send, y_recv, h_send, h_recv, s_send, s_recv,
+):
+    sector, bond = lax.axis_index("sector"), lax.axis_index("mpo")
+    width = left.shape[0]
+    rows = width // chunks
+    pair_rows = rows // 2
+    stacks = bonds // 2
+    core, stack = lax.rem(bond, 2), bond // 2
+    sign = 1 - 2 * lax.rem(sector, 2)
+    partner, ahead, behind = sector + sign, sector + 2 * sign, sector - 2 * sign
+    has_ahead = (ahead >= 0) & (ahead < sectors)
+    has_behind = (behind >= 0) & (behind < sectors)
+    other_core = stack * 2 + 1 - core
+    entries = step_ref.shape[0]
+    peers = sectors * 2
+    me = sector * 2 + core
+
+    def peer_at(step):
+        peer = lax.rem(me + step, peers)
+        return (peer // 2, stack * 2 + lax.rem(peer, 2))
+
+    def stack_at(step):
+        return (sector, lax.rem(stack + step, stacks) * 2 + core)
+
+    load_rows = width // LOADS
+
+    def load(which, n):
+        source, target = ((psi_hbm, psi), (left_hbm, left), (right_hbm, right))[which]
+        here = pl.ds(n * load_rows, load_rows)
+        return pltpu.make_async_copy(source.at[here], target.at[here], in_sem.at[which, n])
+
+    for which in range(3):
+        for n in range(LOADS):
+            load(which, n).start()
+
+    barrier = pltpu.get_barrier_semaphore()
+    for step in range(1, peers):
+        pl.semaphore_signal(barrier, inc=1, device_id=peer_at(step), device_id_type=MESH)
+    for step in range(1, stacks):
+        pl.semaphore_signal(barrier, inc=1, device_id=stack_at(step), device_id_type=MESH)
+
+    def inside(slot):
+        return jnp.minimum(jnp.maximum(slot, 0), sectors - 1)
+
+    own_label = label_ref[sector]
+
+    def couple(source):
+        slot = inside(source)
+        label = label_ref[slot]
+        total = f32(0.0)
+        for entry in range(entries):
+            match = label + step_ref[entry, bond, slot] == own_label
+            value = entry_ref[index_ref[entry, bond, slot]]
+            total = total + jnp.where(match, value, f32(0.0))
+        return jnp.where(source == slot, total, f32(0.0))
+
+    def adjacent(slot):
+        gap = label_ref[inside(slot)] - own_label
+        return (gap == 1) | (gap == -1)
+
+    takes = (jnp.where(adjacent(ahead), f32(1.0), f32(0.0)),
+             jnp.where(adjacent(behind), f32(1.0), f32(0.0)))
+    own_weight = couple(sector)
+    weights = (
+        couple(partner),
+        jnp.where(adjacent(behind), couple(behind), couple(behind + sign)),
+        jnp.where(adjacent(ahead), couple(ahead), couple(ahead + sign)),
+    )
+
+    def send(source, target, send_sem, recv_sem, device):
+        return pltpu.make_async_remote_copy(
+            src_ref=source, dst_ref=target, send_sem=send_sem, recv_sem=recv_sem,
+            device_id=device, device_id_type=MESH,
+        )
+
+    def rows_at(c):
+        return pl.ds(pl.multiple_of(c * rows, rows), rows)
+
+    def block_copy(kind, c):
+        here = rows_at(c)
+        source, device = {
+            FROM_PARTNER: (own, partner),
+            FROM_BELOW: (pick.at[0], ahead),
+            FROM_ABOVE: (pick.at[1], behind),
+        }[kind]
+        return send(
+            source.at[here], slots.at[kind, here], x_send.at[kind, c], x_recv.at[kind, c],
+            (device, bond),
+        )
+
+    sends_if = {FROM_PARTNER: None, FROM_BELOW: has_ahead, FROM_ABOVE: has_behind}
+    gets_if = {FROM_PARTNER: None, FROM_BELOW: has_behind, FROM_ABOVE: has_ahead}
+
+    def when(condition, action):
+        if condition is None:
+            action()
+        else:
+            pl.when(condition)(action)
+
+    def start(kind, c):
+        when(sends_if[kind], lambda: block_copy(kind, c).start())
+
+    def arrive(kind, c):
+        when(gets_if[kind], lambda: block_copy(kind, c).wait_recv())
+
+    def pair_copy(c):
+        there = c * rows + (1 - core) * pair_rows
+        there = pl.ds(pl.multiple_of(there, 8), pair_rows)
+        return send(
+            term.at[there], half_in.at[c], p_send.at[c], p_recv.at[c], (sector, other_core)
+        )
+
+    def half_at(c, which):
+        return pl.ds(pl.multiple_of(c * rows + which * pair_rows, 8), pair_rows)
+
+    def stack_copy(turn, c, step):
+        here = parts.at[turn, stack, c]
+        return send(here, here, y_send.at[c, step - 1], y_recv.at[c, step - 1], stack_at(step))
+
+    def give_pair(turn, c):
+        here = resid.at[turn, half_at(c, core)]
+        return send(here, here, h_send.at[c], h_recv.at[c], (sector, other_core))
+
+    def sum_copy(turn, step):
+        here = sums.at[turn, me]
+        return send(here, here, s_send.at[turn, step - 1], s_recv.at[turn, step - 1], peer_at(step))
+
+    def dots(left_value, right_high, right_low):
+        high, low = split(left_value)
+        dot = functools.partial(jnp.dot, preferred_element_type=f32)
+        count = left_value.shape[0]
+        both_rows = dot(jnp.concatenate([high, low], axis=0), right_high)
+        return both_rows[:count] + (both_rows[count:] + dot(high, right_low))
+
+    def apply(turn, scale):
+        def forward(c):
+            here = rows_at(c)
+            arrive(FROM_PARTNER, c)
+            mine = own[here, :].astype(f32)
+            theirs = slots[FROM_PARTNER, here, :].astype(f32)
+            for kind, take in zip((FROM_BELOW, FROM_ABOVE), takes):
+                value = mine * take + theirs * (1.0 - take)
+                pick[kind - FROM_BELOW, here, :] = value.astype(bf16)
+                start(kind, c)
+
+        def mix(c):
+            here = rows_at(c)
+            arrive(FROM_BELOW, c)
+            arrive(FROM_ABOVE, c)
+            mixed = own_weight * own[here, :].astype(f32)
+            term[here, :] = mixed + weights[0] * slots[FROM_PARTNER, here, :].astype(f32)
+            for kind in (FROM_BELOW, FROM_ABOVE):
+
+                def add(kind=kind):
+                    term[here, :] += weights[kind] * slots[kind, here, :].astype(f32)
+
+                when(gets_if[kind], add)
+            term[here, :] = dots(term[here, :], right_hi[...], right_lo[...])
+            pair_copy(c).start()
+
+        def reduce_pair(c):
+            pair_copy(c).wait_recv()
+            parts[turn, stack, c] = term[half_at(c, core), :] + half_in[c]
+            for step in range(1, stacks):
+                stack_copy(turn, c, step).start()
+
+        def reduce_stack(c):
+            for step in range(1, stacks):
+                stack_copy(turn, c, step).wait_recv()
+            total = parts[turn, 0, c]
+            for place in range(1, stacks):
+                total = total + parts[turn, place, c]
+            here = half_at(c, core)
+            if turn == 0:
+                total = total - coef_ref[0] * psi[here, :]
+            else:
+                total = total - coef_ref[1] * (resid[0, here, :] * scale)
+                total = total - coef_ref[2] * psi[here, :]
+            resid[turn, here, :] = total
+            give_pair(turn, c).start()
+            square = jnp.sum((total * total).reshape(pair_rows // 8, 8, width), axis=0)
+            folded = squares[...]
+            for lane in range(0, width, 128):
+                folded = folded + square[:, lane : lane + 128]
+            squares[...] = folded
+
+            @pl.when(c == chunks - 1)
+            def _():
+                sums[turn, me] = jnp.sum(squares[...], axis=0, keepdims=True)
+                for step in range(1, peers):
+                    sum_copy(turn, step).start()
+
+        def gather(c):
+            give_pair(turn, c).wait_recv()
+            if turn == 0:
+                here = rows_at(c)
+                hi[here, :], lo[here, :] = split(resid[0, here, :])
+
+        stages = [(0, forward), (3, reduce_pair), (2, mix), (5, reduce_stack), (6, gather)]
+
+        def advance(c, carry):
+            for late, action in stages:
+                pl.when((c >= late) & (c < chunks + late))(
+                    functools.partial(action, c - late)
+                )
+            return carry
+
+        squares[...] = jnp.zeros_like(squares)
+        lax.fori_loop(0, chunks + max(late for late, _ in stages), advance, 0)
+
+    def drain_sends(turn):
+        def one(c, carry):
+            for kind in range(3):
+                when(sends_if[kind], lambda kind=kind: block_copy(kind, c).wait_send())
+            pair_copy(c).wait_send()
+            for step in range(1, stacks):
+                stack_copy(turn, c, step).wait_send()
+            give_pair(turn, c).wait_send()
+            return carry
+
+        lax.fori_loop(0, chunks, one, 0)
+
+    def norm(turn):
+        for step in range(1, peers):
+            sum_copy(turn, step).wait_recv()
+        total = jnp.sum(sums[turn], axis=0)
+        total = jnp.sum(total, axis=1, keepdims=True)
+        return 1.0 / jnp.sqrt(total / cells + EPS)
+
+    for n in range(LOADS):
+        here = pl.ds(n * load_rows, load_rows)
+        load(0, n).wait()
+        hi[here, :], lo[here, :] = split(psi[here, :])
+    for n in range(LOADS):
+        here = pl.ds(n * load_rows, load_rows)
+        load(1, n).wait()
+        own[here, :] = dots(left[here, :], hi[...], lo[...]).astype(bf16)
+        if n == 0:
+            pl.semaphore_wait(barrier, peers + stacks - 2)
+        for c in range(n * load_rows // rows, (n + 1) * load_rows // rows):
+            start(FROM_PARTNER, c)
+    for n in range(LOADS):
+        here = pl.ds(n * load_rows, load_rows)
+        load(2, n).wait()
+        right_hi[here, :], right_lo[here, :] = split(right[here, :])
+    apply(0, None)
+
+    drain_sends(0)
+    term[...] = dot_split(left[...], hi[...], lo[...])
+    scale = norm(0)
+
+    def begin(c, carry):
+        here = rows_at(c)
+        own[here, :] = (term[here, :] * scale).astype(bf16)
+        start(FROM_PARTNER, c)
+        return carry
+
+    lax.fori_loop(0, chunks, begin, 0)
+    one_ref[...] = resid[0] * scale
+    apply(1, scale)
+    drain_sends(1)
+    last = norm(1)
+    two_ref[...] = resid[1] * last
+    for turn in range(2):
+        for step in range(1, peers):
+            sum_copy(turn, step).wait_send()
+
+
+def lean_call(sectors, bonds, operands):
+    width = operands[-1].shape[0]
+    chunks = LINK_CHUNKS
+    rows = width // chunks
+    stacks = bonds // 2
+    peers = sectors * 2
+    dma = pltpu.SemaphoreType.DMA
+    smem = pl.BlockSpec(memory_space=pltpu.SMEM)
+    vmem = pl.BlockSpec(memory_space=pltpu.VMEM)
+    whole = pl.BlockSpec(memory_space=pl.ANY)
+    cells = float(sectors * width * width)
+    block = jax.ShapeDtypeStruct((width, width), f32)
+    full_block = pltpu.VMEM((width, width), f32)
+    half_block = pltpu.VMEM((width, width), bf16)
+    return pl.pallas_call(
+        functools.partial(lean_kernel, chunks, sectors, bonds, cells),
+        out_shape=(block, block),
+        in_specs=[smem] * 5 + [whole] * 3,
+        out_specs=(vmem, vmem),
+        scratch_shapes=[
+            full_block, full_block, full_block,
+            half_block, half_block, half_block, half_block, half_block,
+            pltpu.VMEM((2, width, width), bf16),
+            pltpu.VMEM((3, width, width), bf16),
+            full_block,
+            pltpu.VMEM((chunks, rows // 2, width), f32),
+            pltpu.VMEM((2, stacks, chunks, rows // 2, width), f32),
+            pltpu.VMEM((2, width, width), f32),
+            pltpu.VMEM((8, 128), f32),
+            pltpu.VMEM((2, peers, 1, 128), f32),
+            dma((3, LOADS)),
+            dma((3, chunks)), dma((3, chunks)),
+            dma((chunks,)), dma((chunks,)),
+            dma((chunks, stacks - 1)), dma((chunks, stacks - 1)),
+            dma((chunks,)), dma((chunks,)),
+            dma((2, peers - 1)), dma((2, peers - 1)),
+        ],
+        compiler_params=pltpu.CompilerParams(
+            collective_id=1, has_side_effects=True, vmem_limit_bytes=48 * 2**20
+        ),
+        name="lean",
+    )(*operands)
+
+
 def one_block_per_plane(sector_label):
     sectors = sector_label.shape[0]
-    slot = jnp.arange(sectors, dtype=jnp.int32)
-    twin = jnp.where(slot % 2 == 0, jnp.roll(sector_label, -1), jnp.roll(sector_label, 1))
-    adjacent = jnp.abs(sector_label[:, None] - sector_label[None, :]) == 1
-    other = jnp.abs(sector_label[:, None] - twin[None, :]) == 1
-    gap = jnp.abs(slot[:, None] // 2 - slot[None, :] // 2)
-    return ~jnp.any((adjacent & (gap > 1)) | (adjacent & other & (gap == 1)))
+    plane = jnp.arange(sectors, dtype=jnp.int32) // 2
+    upward = sector_label // 2 - plane
+    downward = (sectors - 1 - sector_label) // 2 - plane
+    misses = jnp.sum(jnp.abs(upward) + (jnp.abs(downward) << 16))
+    return ((misses & 0xFFFF) == 0) | ((misses >> 16) == 0)
 
 
 def local(
@@ -377,7 +693,7 @@
     )
     vec_one, vec_two = lax.cond(
         one_block_per_plane(sector_label),
-        lambda: both(True, sectors, bonds, operands),
+        lambda: lean_call(sectors, bonds, operands),
         lambda: both(False, sectors, bonds, operands),
     )
     return (vec_one[None], vec_two[None])

time: 124 us -> 102 us (0.82)
  Pallas kernels: 114 us -> 94.7 us
  local copies, waits for them, and re-layouts: 6.03 us -> 3.91 us
  other arithmetic: 2.81 us -> 1.31 us
    pallas_call x1, Pallas kernels: 114 us -> 94.7 us  [lean_call(): pl.pallas_call(functools.partial(lean_kernel, chunks, sectors, bonds, cel...]
    slice x2 -> x0, local copies, waits for them, and re-layouts: 2.12 us -> none  [one_block_per_plane(): jnp.roll(sector_label, 1)]
    reduce_or x1 -> x0, other arithmetic: 1.45 us -> none  [one_block_per_plane(): return ~jnp.any(adjacent & (gap > 1) | adjacent & other & (gap == 1))]
    select_n x1 -> x0, other arithmetic: 1.37 us -> none  [one_block_per_plane(): jnp.where(slot % 2 == 0, jnp.roll(sector_label, -1), jnp.roll(sector_labe...]
    reduce_sum x0 -> x1, other arithmetic: none -> 1.31 us  [one_block_per_plane(): misses = jnp.sum(jnp.abs(upward) + (jnp.abs(downward) << 16))]
where the time goes in v1:
time: 102 us
  Pallas kernels  94.7 us (93%)
  local copies, waits for them, and re-layouts  3.91 us (4%)
  between operations  1.95 us (2%)
  other arithmetic  1.31 us (1%)
    pallas_call x1, Pallas kernels, lean_call(): pl.pallas_call(functools.partial(lean_kernel, chunks, sectors, bonds, cel...  94.7 us
    unnamed x4, local copies, waits for them, and re-layouts  3.91 us

profile of v1, /device:TPU:0, one launch (start us, length us, event | category | flops | bytes accessed | tf_op | source)
XLA Modules:
  0.0 102.1 jit_solution(2823545208083310456)
XLA Ops:
  0.6 1.3 %add_reduce_fusion = s32[]{:T(128)} fusion(s32[8]{0:T(128)} %param.13), kind=kLoop, calls=%fused_computation.12 | loop fusion | flops 367 | bytes 36 | tf_op jit(solution)/shard_map/reduce_sum | solution.py:682
  3.2 94.9 %conditional.1 = ((f32[768,768]{1,0:T(8,128)S(1)}, f32[768,768]{1,0:T(8,128)})) conditional(s32[]{:T(128)} %convert_element_type.3, (s32[8]{0:T(128)}, s32[3,4,8]{2,1,0:T(4,128)}, s32[3,4,8]{2,1,0:T(4,128)}, f32[8]{0:T(128)}, f32[3]{0:T(128)}, /*index=5*/f32[768,768]{1,0:T(8,128)}, f32[768,768]{1,0:T(8,128)}, f32[768,768]{1,0:T(8,128)}) %tuple.37, ...), branch_computations={%region_1.2_spmd, %region_2.3_spmd} | conditional | bytes 8 | solution.py:694
  3.4 94.7 %lean.1 = (f32[768,768]{1,0:T(8,128)S(1)}, f32[768,768]{1,0:T(8,128)}) custom-call(s32[8]{0:T(128)} %get-tuple-element.48.label_ref, s32[3,4,8]{2,1,0:T(4,128)} %get-tuple-element.49.step_ref, s32[3,4,8]{2,1,0:T(4,128)} %get-tuple-element.50.index_ref, f32[8]{0:T(128)} %get-tuple-element.51.entry_ref, f32[3]{0:T(128)} %get-tuple-element.52.coef_ref, ...), custom_call_target="tpu_custom_call" | custom-call | tf_op jit(solution)/shard_map/cond/branch_1_fun/lean/pallas_call | solution.py:647
  98.2 0.0 copy-start
  98.2 1.4 %copy.16 = f32[1,768,768]{2,1,0:T(8,128)} copy(f32[1,768,768]{2,1,0:T(8,128)S(1)} %bitcast.13) | data formatting | bytes 4718592
  99.6 1.1 %copy-done = f32[768,768]{1,0:T(8,128)S(1)} copy-done((f32[768,768]{1,0:T(8,128)S(1)}, f32[768,768]{1,0:T(8,128)}, u32[]{:S(2)}) %copy-start) | copy-done | bytes 2359320
  100.7 1.4 %copy.17 = f32[1,768,768]{2,1,0:T(8,128)} copy(f32[1,768,768]{2,1,0:T(8,128)S(1)} %bitcast.14) | data formatting | bytes 4718592
Async XLA Ops:
  98.2 2.5 %copy-start = (f32[768,768]{1,0:T(8,128)S(1)}, f32[768,768]{1,0:T(8,128)}, u32[]{:S(2)}) copy-start(f32[768,768]{1,0:T(8,128)} %get-tuple-element.61) | copy-start | bytes 7077892

commit v2 on v1

--- a/solution.py
+++ b/solution.py
@@ -8,7 +8,7 @@
 from jax.sharding import PartitionSpec as P
 
 EPS = 1e-06
-LINK_CHUNKS, FULL_CHUNKS, LOADS = 12, 3, 6
+LINK_CHUNKS, FULL_CHUNKS, LOADS = 16, 3, 4
 FROM_PARTNER, FROM_BELOW, FROM_ABOVE, PARTNER_RELAY, ABOVE_RELAY, BELOW_RELAY = range(6)
 MESH = pl.DeviceIdType.MESH
 f32, bf16 = jnp.float32, jnp.bfloat16
@@ -351,7 +351,7 @@
             dma((2, sectors - 1)), dma((2, sectors - 1)),
         ],
         compiler_params=pltpu.CompilerParams(
-            collective_id=int(lean), has_side_effects=True, vmem_limit_bytes=60 * 2**20
+            collective_id=int(lean), has_side_effects=True, vmem_limit_bytes=42 * 2**20
         ),
         name="lean" if lean else "full",
     )(*operands)
@@ -359,10 +359,10 @@
 
 def lean_kernel(
     chunks, sectors, bonds, cells,
-    label_ref, step_ref, index_ref, entry_ref, coef_ref, left_hbm, right_hbm, psi_hbm,
+    label_hbm, step_hbm, index_hbm, entry_hbm, coef_hbm, left_hbm, right_hbm, psi_hbm,
     one_ref, two_ref,
-    left, right, psi, hi, lo, right_hi, right_lo, own, pick, slots, term, half_in, parts, resid, squares, sums,
-    in_sem, x_send, x_recv, p_send, p_recv, y_send, y_recv, h_send, h_recv, s_send, s_recv,
+    label_ref, step_ref, index_ref, entry_ref, coef_ref, left, right, psi, hi, lo, right_hi, right_lo, own, pick, slots, term, half_in, parts, resid, squares, sums,
+    in_sem, small_sem, x_send, x_recv, p_send, p_recv, y_send, y_recv, h_send, h_recv, s_send, s_recv,
 ):
     sector, bond = lax.axis_index("sector"), lax.axis_index("mpo")
     width = left.shape[0]
@@ -397,39 +397,30 @@
         for n in range(LOADS):
             load(which, n).start()
 
+    smalls = [
+        pltpu.make_async_copy(source, target, small_sem.at[n])
+        for n, (source, target) in enumerate((
+            (label_hbm, label_ref), (step_hbm, step_ref), (index_hbm, index_ref),
+            (entry_hbm, entry_ref), (coef_hbm, coef_ref),
+        ))
+    ]
+    for small in smalls:
+        small.start()
     barrier = pltpu.get_barrier_semaphore()
-    for step in range(1, peers):
-        pl.semaphore_signal(barrier, inc=1, device_id=peer_at(step), device_id_type=MESH)
+
+    def greet(device):
+        pl.semaphore_signal(barrier, inc=1, device_id=device, device_id_type=MESH)
+
+    greet((partner, bond))
+    greet((sector, other_core))
     for step in range(1, stacks):
-        pl.semaphore_signal(barrier, inc=1, device_id=stack_at(step), device_id_type=MESH)
+        greet(stack_at(step))
+    pl.when(has_ahead)(lambda: greet((ahead, bond)))
+    pl.when(has_behind)(lambda: greet((behind, bond)))
+    greetings = 1 + stacks + has_ahead.astype(jnp.int32) + has_behind.astype(jnp.int32)
 
     def inside(slot):
         return jnp.minimum(jnp.maximum(slot, 0), sectors - 1)
-
-    own_label = label_ref[sector]
-
-    def couple(source):
-        slot = inside(source)
-        label = label_ref[slot]
-        total = f32(0.0)
-        for entry in range(entries):
-            match = label + step_ref[entry, bond, slot] == own_label
-            value = entry_ref[index_ref[entry, bond, slot]]
-            total = total + jnp.where(match, value, f32(0.0))
-        return jnp.where(source == slot, total, f32(0.0))
-
-    def adjacent(slot):
-        gap = label_ref[inside(slot)] - own_label
-        return (gap == 1) | (gap == -1)
-
-    takes = (jnp.where(adjacent(ahead), f32(1.0), f32(0.0)),
-             jnp.where(adjacent(behind), f32(1.0), f32(0.0)))
-    own_weight = couple(sector)
-    weights = (
-        couple(partner),
-        jnp.where(adjacent(behind), couple(behind), couple(behind + sign)),
-        jnp.where(adjacent(ahead), couple(ahead), couple(ahead + sign)),
-    )
 
     def send(source, target, send_sem, recv_sem, device):
         return pltpu.make_async_remote_copy(
@@ -600,13 +591,40 @@
         load(1, n).wait()
         own[here, :] = dots(left[here, :], hi[...], lo[...]).astype(bf16)
         if n == 0:
-            pl.semaphore_wait(barrier, peers + stacks - 2)
+            pl.semaphore_wait(barrier, greetings)
         for c in range(n * load_rows // rows, (n + 1) * load_rows // rows):
             start(FROM_PARTNER, c)
     for n in range(LOADS):
         here = pl.ds(n * load_rows, load_rows)
         load(2, n).wait()
         right_hi[here, :], right_lo[here, :] = split(right[here, :])
+    for small in smalls:
+        small.wait()
+    own_label = label_ref[sector]
+
+    def couple(source):
+        slot = inside(source)
+        label = label_ref[slot]
+        total = f32(0.0)
+        for entry in range(entries):
+            match = label + step_ref[entry, bond, slot] == own_label
+            value = entry_ref[index_ref[entry, bond, slot]]
+            total = total + jnp.where(match, value, f32(0.0))
+        return jnp.where(source == slot, total, f32(0.0))
+
+    def adjacent(slot):
+        gap = label_ref[inside(slot)] - own_label
+        return (gap == 1) | (gap == -1)
+
+    takes = (jnp.where(adjacent(ahead), f32(1.0), f32(0.0)),
+             jnp.where(adjacent(behind), f32(1.0), f32(0.0)))
+    own_weight = couple(sector)
+    weights = (
+        couple(partner),
+        jnp.where(adjacent(behind), couple(behind), couple(behind + sign)),
+        jnp.where(adjacent(ahead), couple(ahead), couple(ahead + sign)),
+    )
+
     apply(0, None)
 
     drain_sends(0)
@@ -637,7 +655,6 @@
     stacks = bonds // 2
     peers = sectors * 2
     dma = pltpu.SemaphoreType.DMA
-    smem = pl.BlockSpec(memory_space=pltpu.SMEM)
     vmem = pl.BlockSpec(memory_space=pltpu.VMEM)
     whole = pl.BlockSpec(memory_space=pl.ANY)
     cells = float(sectors * width * width)
@@ -647,9 +664,10 @@
     return pl.pallas_call(
         functools.partial(lean_kernel, chunks, sectors, bonds, cells),
         out_shape=(block, block),
-        in_specs=[smem] * 5 + [whole] * 3,
+        in_specs=[whole] * 8,
         out_specs=(vmem, vmem),
         scratch_shapes=[
+            *(pltpu.SMEM(small.shape, small.dtype) for small in operands[:5]),
             full_block, full_block, full_block,
             half_block, half_block, half_block, half_block, half_block,
             pltpu.VMEM((2, width, width), bf16),
@@ -660,7 +678,7 @@
             pltpu.VMEM((2, width, width), f32),
             pltpu.VMEM((8, 128), f32),
             pltpu.VMEM((2, peers, 1, 128), f32),
-            dma((3, LOADS)),
+            dma((3, LOADS)), dma((5,)),
             dma((3, chunks)), dma((3, chunks)),
             dma((chunks,)), dma((chunks,)),
             dma((chunks, stacks - 1)), dma((chunks, stacks - 1)),
@@ -668,7 +686,7 @@
             dma((2, peers - 1)), dma((2, peers - 1)),
         ],
         compiler_params=pltpu.CompilerParams(
-            collective_id=1, has_side_effects=True, vmem_limit_bytes=48 * 2**20
+            collective_id=1, has_side_effects=True, vmem_limit_bytes=42 * 2**20
         ),
         name="lean",
     )(*operands)

time: 102 us -> 97.4 us (0.955)
  Pallas kernels: 94.7 us -> 91 us
  local copies, waits for them, and re-layouts: 3.91 us -> 2.81 us
    pallas_call x1, Pallas kernels: 94.7 us -> 91 us  [lean_call(): pl.pallas_call(functools.partial(lean_kernel, chunks, sectors, bonds, cel...]
    unnamed x4 -> x2, local copies, waits for them, and re-layouts: 3.91 us -> 2.81 us
where the time goes in v2:
time: 97.4 us; the launch traced here: 97.3 us
  Pallas kernels  91 us (93%)
  local copies, waits for them, and re-layouts  2.81 us (3%)
  between operations  1.94 us (2%)
  other arithmetic  1.31 us (1%)
    pallas_call x1, Pallas kernels, lean_call(): pl.pallas_call(functools.partial(lean_kernel, chunks, sectors, bonds, cel...  91 us
    unnamed x2, local copies, waits for them, and re-layouts  2.81 us

profile of v2, /device:TPU:0, one launch (start us, length us, event | category | flops | bytes accessed | tf_op | source)
XLA Modules:
  0.0 97.3 jit_solution(11634574447379967978)
XLA Ops:
  0.6 1.3 %add_reduce_fusion = s32[]{:T(128)} fusion(s32[8]{0:T(128)} %param.13), kind=kLoop, calls=%fused_computation.12 | loop fusion | flops 367 | bytes 36 | tf_op jit(solution)/shard_map/reduce_sum | solution.py:700
  3.2 91.2 %conditional.1 = ((f32[768,768]{1,0:T(8,128)S(1)}, f32[768,768]{1,0:T(8,128)S(1)})) conditional(s32[]{:T(128)} %convert_element_type.3, (s32[8]{0:T(128)}, s32[3,4,8]{2,1,0:T(4,128)}, s32[3,4,8]{2,1,0:T(4,128)}, f32[8]{0:T(128)}, f32[3]{0:T(128)}, /*index=5*/f32[768,768]{1,0:T(8,128)}, f32[768,768]{1,0:T(8,128)}, f32[768,768]{1,0:T(8,128)}) %tuple.37, ...), branch_computations={%region_1.2_spmd, %region_2.3_spmd} | conditional | bytes 8 | solution.py:712
  3.3 91.0 %lean.1 = (f32[768,768]{1,0:T(8,128)S(1)}, f32[768,768]{1,0:T(8,128)S(1)}) custom-call(s32[8]{0:T(128)} %get-tuple-element.48.label_hbm, s32[3,4,8]{2,1,0:T(4,128)} %get-tuple-element.49.step_hbm, s32[3,4,8]{2,1,0:T(4,128)} %get-tuple-element.50.index_hbm, f32[8]{0:T(128)} %get-tuple-element.51.entry_hbm, f32[3]{0:T(128)} %get-tuple-element.52.coef_hbm, ...), custom_call_target="tpu_custom_call" | custom-call | tf_op jit(solution)/shard_map/cond/branch_1_fun/lean/pallas_call | solution.py:664
  94.5 1.4 %copy.16 = f32[1,768,768]{2,1,0:T(8,128)} copy(f32[1,768,768]{2,1,0:T(8,128)S(1)} %bitcast.13) | data formatting | bytes 4718592
  95.9 1.4 %copy.17 = f32[1,768,768]{2,1,0:T(8,128)} copy(f32[1,768,768]{2,1,0:T(8,128)S(1)} %bitcast.14) | data formatting | bytes 4718592
